TPU v7x, 32 devices: a whole 2x2x4 slice. The times are simulated.
32 devices in a mesh: cell: 8 (over z, x), desc: 4 (over y, core).
Axes of the slice: x: 2, y: 2, z: 4, core: 2. Of those that a mesh axis runs over, the one named last changes fastest.
Arguments:
- cells: float32 [8192, 256], P('cell'), may hold values from -128 to 128
- descs: float32 [8192, 256], P('desc'), may hold values from -4 to 4
- g_start: float32 [8192], P('desc'), may hold values from -8 to 8
- cot_f: float32 [8192], P('cell'), may hold values from -24 to 24
- cot_g: float32 [8192], P('desc'), may hold values from -24 to 24
Outputs:
- grad_cells: float32 [8192, 256], P('cell')
- grad_descs: float32 [8192, 256], P('desc')
All inputs are finite; a program needn't handle non-finite values.
Results may differ from a plain program's by a relative error of at most 0.0003.
Values sent between devices are 32-bit elements; how exact they have to be, the bound alone decides.
A program may use at most 192 MiB of HBM per device.

v0:
```python
import math
import jax
import jax.numpy as jnp
from jax import lax
from jax.sharding import PartitionSpec as P

ITERS = 4


def combined_all(value, axis, join):
    pieces = jax.tree.map(lambda part: lax.all_gather(part, axis), value)
    head = jax.tree.map(lambda part: part[0], pieces)
    tail = jax.tree.map(lambda part: part[1:], pieces)
    so_far, _ = lax.scan(lambda so_far, share: (join(so_far, share), None), head, tail)
    return so_far


def lse_merge(first, second):
    max_one, sum_one = first
    max_two, sum_two = second
    top = jnp.maximum(max_one, max_two)
    return (top, sum_one * jnp.exp(max_one - top) + sum_two * jnp.exp(max_two - top))


def plan_adjoint(xrows, ycols, g_first, cf_rows, cg_cols, over_rows, over_cols, sum_rows, sum_cols):
    scale = 2.0 / math.sqrt(xrows.shape[1])
    highest = lax.Precision.HIGHEST
    logit = (
        lax.dot_general(
            xrows,
            ycols,
            (((1,), (1,)), ((), ())),
            precision=highest,
            preferred_element_type=jnp.float32,
        )
        * scale
    )
    g_now = g_first
    f_list = []
    g_list = [g_first]
    for step in range(ITERS):
        zvals = logit + g_now[None, :]
        row_max = jnp.max(zvals, axis=1)
        row_sum = jnp.sum(jnp.exp(zvals - row_max[:, None]), axis=1)
        row_max, row_sum = over_rows(row_max, row_sum)
        f_now = -(row_max + jnp.log(row_sum))
        wvals = logit + f_now[:, None]
        col_max = jnp.max(wvals, axis=0)
        col_sum = jnp.sum(jnp.exp(wvals - col_max[None, :]), axis=0)
        col_max, col_sum = over_cols(col_max, col_sum)
        g_now = -(col_max + jnp.log(col_sum))
        f_list.append(f_now)
        g_list.append(g_now)
    gbar = cg_cols
    lbar = jnp.zeros_like(logit)
    for step in reversed(range(ITERS)):
        g_here = g_list[step + 1]
        bplan = jnp.exp(logit + f_list[step][:, None] + g_here[None, :])
        fbar = -sum_rows(jnp.sum(bplan * gbar[None, :], axis=1))
        if step == ITERS - 1:
            fbar = fbar + cf_rows
        aplan = bplan * jnp.exp(g_list[step] - g_here)[None, :]
        lbar = lbar - (bplan * gbar[None, :] + aplan * fbar[:, None])
        if step > 0:
            gbar = -sum_cols(jnp.sum(aplan * fbar[:, None], axis=0))
    return (lbar, scale)


def on_device(cells, descs, g_start, cot_f, cot_g):
    highest = lax.Precision.HIGHEST
    lbar, scale = plan_adjoint(
        cells,
        descs,
        g_start,
        cot_f,
        cot_g,
        lambda big, total: combined_all((big, total), "desc", lse_merge),
        lambda big, total: combined_all((big, total), "cell", lse_merge),
        lambda part: lax.psum(part, "desc"),
        lambda part: lax.psum(part, "cell"),
    )
    part_x = scale * jnp.dot(lbar, descs, precision=highest, preferred_element_type=jnp.float32)
    part_y = scale * lax.dot_general(
        lbar, cells, (((0,), (0,)), ((), ())), precision=highest, preferred_element_type=jnp.float32
    )
    grad_cells = lax.psum(part_x, "desc")
    grad_descs = lax.psum(part_y, "cell")
    return (grad_cells, grad_descs)


def solution(mesh):
    placed = (P("cell", None), P("desc", None), P("desc"), P("cell"), P("desc"))
    return jax.shard_map(
        on_device,
        mesh=mesh,
        in_specs=placed,
        out_specs=(P("cell", None), P("desc", None)),
        check_vma=False,
    )
```

profile of v0, /device:TPU:0, one launch (start us, length us, event | category | flops | bytes accessed | tf_op | source)
XLA Modules:
  0.0 670.6 jit_solution(9534914086355051639)
XLA Ops:
  8.8 9.0 %add_reduce_fusion.3 = (f32[1024]{0:T(1024)S(1)}, f32[1024,2048]{1,0:T(8,128)S(1)}) fusion(f32[2048]{0:T(1024)} %param.23, f32[1024,256]{1,0:T(8,128)} %param.21, f32[2048,256]{1,0:T(8,128)S(1)} %copy-done), kind=kOutput, calls=%fused_computation.47 | convolution fusion | flops 6448741376 | bytes 11546624 | tf_op jit(solution)/shard_map/dot_general | solution.py:29
  17.8 6.3 all-gather
  26.1 5.4 all-gather.1
  31.7 4.2 add_reduce_fusion.7
  39.3 31.1 %all-gather.2 = f32[16384]{0:T(1024)S(1)} all-gather(f32[2048]{0:T(1024)S(1)} %add_reduce_fusion.7), channel_id=4, replica_groups=mesh['cell'=8,'desc'=4] {'cell'}, dimensions={0}, use_global_device_ids=true | all-gather | bytes 73728 | tf_op jit(solution)/shard_map/all_gather | solution.py:11
  70.3 30.7 %all-gather.3 = f32[16384]{0:T(1024)S(1)} all-gather(f32[2048]{0:T(1024)S(1)} %exponential_reduce_fusion.6), channel_id=5, replica_groups=mesh['cell'=8,'desc'=4] {'cell'}, dimensions={0}, use_global_device_ids=true | all-gather | bytes 73728 | tf_op jit(solution)/shard_map/all_gather | solution.py:11
  101.6 4.0 add_reduce_fusion.2
  105.6 4.4 exponential_reduce_fusion.5
  109.9 5.2 all-gather.4
  115.1 5.2 all-gather.5
  120.5 4.0 add_reduce_fusion.6
  124.5 4.3 exponential_reduce_fusion.4
  128.9 30.5 %all-gather.6 = f32[16384]{0:T(1024)S(1)} all-gather(f32[2048]{0:T(1024)S(1)} %add_reduce_fusion.6), channel_id=8, replica_groups=mesh['cell'=8,'desc'=4] {'cell'}, dimensions={0}, use_global_device_ids=true | all-gather | bytes 73728 | tf_op jit(solution)/shard_map/all_gather | solution.py:11
  159.4 30.5 %all-gather.7 = f32[16384]{0:T(1024)S(1)} all-gather(f32[2048]{0:T(1024)S(1)} %exponential_reduce_fusion.4), channel_id=9, replica_groups=mesh['cell'=8,'desc'=4] {'cell'}, dimensions={0}, use_global_device_ids=true | all-gather | bytes 73728 | tf_op jit(solution)/shard_map/all_gather | solution.py:11
  194.5 4.4 exponential_reduce_fusion.3
  198.8 5.2 all-gather.8
  204.0 5.2 all-gather.9
  209.4 4.0 add_reduce_fusion.5
  213.4 4.3 exponential_reduce_fusion.2
  217.8 30.5 %all-gather.10 = f32[16384]{0:T(1024)S(1)} all-gather(f32[2048]{0:T(1024)S(1)} %add_reduce_fusion.5), channel_id=12, replica_groups=mesh['cell'=8,'desc'=4] {'cell'}, dimensions={0}, use_global_device_ids=true | all-gather | bytes 73728 | tf_op jit(solution)/shard_map/all_gather | solution.py:11
  248.3 30.5 %all-gather.11 = f32[16384]{0:T(1024)S(1)} all-gather(f32[2048]{0:T(1024)S(1)} %exponential_reduce_fusion.2), channel_id=13, replica_groups=mesh['cell'=8,'desc'=4] {'cell'}, dimensions={0}, use_global_device_ids=true | all-gather | bytes 73728 | tf_op jit(solution)/shard_map/all_gather | solution.py:11
  279.3 4.0 add_reduce_fusion
  283.4 4.4 exponential_reduce_fusion.1
  287.8 5.2 all-gather.12
  293.0 5.4 all-gather.13
  298.6 4.0 add_reduce_fusion.4
  302.6 4.3 exponential_reduce_fusion
  306.9 30.5 %all-gather.14 = f32[16384]{0:T(1024)S(1)} all-gather(f32[2048]{0:T(1024)S(1)} %add_reduce_fusion.4), channel_id=16, replica_groups=mesh['cell'=8,'desc'=4] {'cell'}, dimensions={0}, use_global_device_ids=true | all-gather | bytes 73728 | tf_op jit(solution)/shard_map/all_gather | solution.py:11
  337.5 30.5 %all-gather.15 = f32[16384]{0:T(1024)S(1)} all-gather(f32[2048]{0:T(1024)S(1)} %exponential_reduce_fusion), channel_id=17, replica_groups=mesh['cell'=8,'desc'=4] {'cell'}, dimensions={0}, use_global_device_ids=true | all-gather | bytes 73728 | tf_op jit(solution)/shard_map/all_gather | solution.py:11
  368.5 4.5 multiply_reduce_fusion.3
  373.1 5.7 psum.63
  378.7 4.7 fusion
  383.4 21.5 %psum.64 = f32[2048]{0:T(1024)S(1)} all-reduce(f32[2048]{0:T(1024)S(1)} %fusion), channel_id=1, replica_groups=mesh['cell'=8,'desc'=4] {'cell'}, use_global_device_ids=true, to_apply=%region_35.36 | all-reduce | flops 2048 | bytes 16384 | tf_op jit(solution)/shard_map/psum | solution.py:80
  404.9 4.5 multiply_reduce_fusion.2
  409.4 5.7 psum.65
  415.1 4.6 fusion.1
  419.7 17.4 %psum.66 = f32[2048]{0:T(1024)S(1)} all-reduce(f32[2048]{0:T(1024)S(1)} %fusion.1), channel_id=1, replica_groups=mesh['cell'=8,'desc'=4] {'cell'}, use_global_device_ids=true, to_apply=%region_39.40 | all-reduce | flops 2048 | bytes 16384 | tf_op jit(solution)/shard_map/psum | solution.py:80
  437.1 4.5 multiply_reduce_fusion.1
  441.7 5.7 psum.67
  447.3 4.6 fusion.2
  452.0 19.4 %psum.68 = f32[2048]{0:T(1024)S(1)} all-reduce(f32[2048]{0:T(1024)S(1)} %fusion.2), channel_id=1, replica_groups=mesh['cell'=8,'desc'=4] {'cell'}, use_global_device_ids=true, to_apply=%region_43.44 | all-reduce | flops 2048 | bytes 16384 | tf_op jit(solution)/shard_map/psum | solution.py:80
  471.4 4.5 multiply_reduce_fusion
  475.9 6.1 psum.69
  482.0 24.1 %add_subtract_fusion = f32[1024,2048]{1,0:T(8,128)S(1)} fusion(f32[1024,2048]{1,0:T(8,128)} %copy-done.1, f32[1024]{0:T(1024)S(1)} %neg.59, f32[2048]{0:T(1024)S(1)} %get-tuple-element.338, f32[2048]{0:T(1024)S(1)} %neg.58, f32[1024]{0:T(1024)S(1)} %neg.57, f32[2048]{0:T(1024)S(1)} %get-tuple-element.340, f32[2048]{0:T(1024)S(1)} %neg.56, f32[1024]{0:T(1024)S(1)} %neg.55, ...), kind=kLoop, calls=%fused_computation.24 | loop fusion | flops 58720256 | bytes 16908288 | tf_op jit(solution)/shard_map/sub | solution.py:63
  509.3 7.6 %convolution_multiply_fusion.2 = f32[1024,256]{1,0:T(8,128)} fusion(f32[1024,2048]{1,0:T(8,128)S(1)} %add_subtract_fusion, f32[2048,256]{1,0:T(8,128)S(1)} %copy-done), kind=kOutput, calls=%fused_computation.57 | convolution fusion | flops 6442713088 | bytes 11534336 | tf_op jit(solution)/shard_map/dot_general | solution.py:82
  517.2 16.5 %convolution_multiply_fusion.1 = f32[2048,256]{1,0:T(8,128)} fusion(f32[1024,2048]{1,0:T(8,128)} %copy-done.3, f32[1024,256]{1,0:T(8,128)S(1)} %copy-done.4), kind=kOutput, calls=%fused_computation.56 | convolution fusion | flops 6442975232 | bytes 11534336 | tf_op jit(solution)/shard_map/dot_general | solution.py:83
  533.7 17.5 %all-reduce.3.cloned.1.call-done = f32[1024,256]{1,0:T(8,128)} async-done(((f32[1024,256]{1,0:T(8,128)}), f32[1024,256]{1,0:T(8,128)}) %all-reduce.3.cloned.1.call-update) | async-done | bytes 1048592 | tf_op jit(solution)/shard_map/psum | solution.py:86
  551.3 107.0 %all-reduce.5.cloned.1.call-done = f32[2048,256]{1,0:T(8,128)} async-done(((f32[2048,256]{1,0:T(8,128)}), f32[2048,256]{1,0:T(8,128)}) %all-reduce.5.cloned.1.call-update) | async-done | bytes 2097168 | tf_op jit(solution)/shard_map/psum | solution.py:87
  (176 shorter events, 23.6 us)
Async XLA Ops:
  7.2 1.6 copy-start
  7.2 16.9 %copy-start.5 = (f32[2048]{0:T(1024)S(1)}, f32[2048]{0:T(1024)}, u32[]{:S(2)}) copy-start(f32[2048]{0:T(1024)} %param.23) | copy-start | bytes 24580
  7.2 544.1 %all-reduce.3.cloned.1.call-start = ((), (), s32[]{:S(2)}) async-start(), calls=%async_computation | async-start | bytes 2097152 | tf_op jit(solution)/shard_map/psum | solution.py:86
  17.8 6.3 copy-start.1
  31.7 5.8 copy-start.2
  298.6 69.9 %copy-start.6 = (f32[2048]{0:T(1024)S(1)}, f32[2048]{0:T(1024)}, u32[]{:S(2)}) copy-start(f32[2048]{0:T(1024)} %param.25) | copy-start | bytes 24580
  302.6 76.1 %copy-start.7 = (f32[1024]{0:T(1024)S(1)}, f32[1024]{0:T(1024)}, u32[]{:S(2)}) copy-start(f32[1024]{0:T(1024)} %param.24) | copy-start | bytes 12292
  506.1 3.2 copy-start.3
  509.3 7.9 %copy-start.4 = (f32[1024,256]{1,0:T(8,128)S(1)}, f32[1024,256]{1,0:T(8,128)}, u32[]{:S(2)}) copy-start(f32[1024,256]{1,0:T(8,128)} %param.21) | copy-start | bytes 3145732
  516.9 141.3 %all-reduce.5.cloned.1.call-start = ((), (), s32[]{:S(2)}) async-start(), calls=%async_computation.1 | async-start | bytes 4194304 | tf_op jit(solution)/shard_map/psum | solution.py:87
Sparse Core Ops, SparseCore 0:
  517.1 34.1 all-reduce.2
  555.5 102.7 all-reduce.4
where the time goes:
time: 679 us; the launch traced here: 671 us
  blocking collectives  369 us (54%)
  waiting for transfers between devices  125 us (18%)
  other arithmetic  115 us (17%)
  matrix products  33.2 us (5%)
  between operations  14.7 us (2%)
  local copies, waits for them, and re-layouts  12.6 us (2%)
    all_gather x16, blocking collectives, combined_all(): pieces = jax.tree.map(lambda part: lax.all_gather(part, axis), value)  288 us
    psum x1, waiting for transfers between devices, on_device(): grad_descs = lax.psum(part_y, 'cell')  107 us
    psum x3, blocking collectives, on_device(): lax.psum(part, 'cell')  58.3 us
    sub x1, other arithmetic, plan_adjoint(): lbar = lbar - (bplan * gbar[None, :] + aplan * fbar[:, None])  24.1 us
    psum x4, blocking collectives, on_device(): lax.psum(part, 'desc')  23.1 us
    reduce_sum x4, other arithmetic, plan_adjoint(): fbar = -sum_rows(jnp.sum(bplan * gbar[None, :], axis=1))  18.1 us
    psum x1, waiting for transfers between devices, on_device(): grad_cells = lax.psum(part_x, 'desc')  17.5 us
    dot_general x1, matrix products, on_device(): lax.dot_general(lbar, cells, (((0,), (0,)), ((), ())), precision=highest,...  16.5 us
  transfers between devices with their start and end apart: 2, of which 2 were waited for; matrix products, arithmetic and copies ran while one was open for 2% of the time, Pallas kernels for 0%

commit v1 on v0

--- a/solution.py
+++ b/solution.py
@@ -84,7 +84,11 @@
         lbar, cells, (((0,), (0,)), ((), ())), precision=highest, preferred_element_type=jnp.float32
     )
     grad_cells = lax.psum(part_x, "desc")
-    grad_descs = lax.psum(part_y, "cell")
+    grad_descs = part_y
+    for hop in (1, 2, 4):
+        grad_descs = grad_descs + lax.ppermute(
+            grad_descs, "cell", [(dev, dev ^ hop) for dev in range(8)]
+        )
     return (grad_cells, grad_descs)
 
 

time: 679 us -> 730 us (1.075)
  waiting for transfers between devices: 125 us -> 179 us
    ppermute x0 -> x3, waiting for transfers between devices: none -> 179 us  [on_device(): lax.ppermute(grad_descs, 'cell', [(dev, dev ^ hop) for dev in range(8)])]
    psum x1 -> x0, waiting for transfers between devices: 107 us -> none  [on_device(): grad_descs = lax.psum(part_y, 'cell')]
    psum x1, waiting for transfers between devices: 17.5 us -> 0.01 us  [on_device(): grad_cells = lax.psum(part_x, 'desc')]
  transfers between devices with their start and end apart: 2 -> 4, of which waited for: 2 -> 3; matrix products, arithmetic and copies ran while one was open for 2% -> 2% of each run, Pallas kernels for 0% -> 0%
where the time goes in v1:
time: 730 us; the launch traced here: 722 us
  blocking collectives  369 us (51%)
  waiting for transfers between devices  179 us (25%)
  other arithmetic  121 us (17%)
  matrix products  30.1 us (4%)
  between operations  14.7 us (2%)
    all_gather x16, blocking collectives, combined_all(): pieces = jax.tree.map(lambda part: lax.all_gather(part, axis), value)  288 us
    ppermute x3, waiting for transfers between devices, on_device(): lax.ppermute(grad_descs, 'cell', [(dev, dev ^ hop) for dev in range(8)])  179 us
    psum x3, blocking collectives, on_device(): lax.psum(part, 'cell')  58.3 us
    sub x1, other arithmetic, plan_adjoint(): lbar = lbar - (bplan * gbar[None, :] + aplan * fbar[:, None])  24.6 us
    psum x4, blocking collectives, on_device(): lax.psum(part, 'desc')  22.7 us
    reduce_sum x4, other arithmetic, plan_adjoint(): fbar = -sum_rows(jnp.sum(bplan * gbar[None, :], axis=1))  18.1 us
    reduce_max x4, other arithmetic, plan_adjoint(): col_max = jnp.max(wvals, axis=0)  16.2 us
    reduce_sum x4, other arithmetic, plan_adjoint(): row_sum = jnp.sum(jnp.exp(zvals - row_max[:, None]), axis=1)  15.1 us
  transfers between devices with their start and end apart: 4, of which 3 were waited for; matrix products, arithmetic and copies ran while one was open for 2% of the time, Pallas kernels for 0%

profile of v1, /device:TPU:0, one launch (start us, length us, event | category | flops | bytes accessed | tf_op | source)
XLA Modules:
  0.0 721.8 jit_solution(7140182591552215706)
XLA Ops:
  8.8 9.0 %add_reduce_fusion.3 = (f32[1024]{0:T(1024)S(1)}, f32[1024,2048]{1,0:T(8,128)S(1)}) fusion(f32[2048]{0:T(1024)} %param.23, f32[1024,256]{1,0:T(8,128)} %param.21, f32[2048,256]{1,0:T(8,128)S(1)} %copy-done), kind=kOutput, calls=%fused_computation.47 | convolution fusion | flops 6448741376 | bytes 11546624 | tf_op jit(solution)/shard_map/dot_general | solution.py:29
  17.8 6.3 all-gather
  26.1 5.4 all-gather.1
  31.7 4.2 add_reduce_fusion.7
  39.3 31.1 %all-gather.2 = f32[16384]{0:T(1024)S(1)} all-gather(f32[2048]{0:T(1024)S(1)} %add_reduce_fusion.7), channel_id=4, replica_groups=mesh['cell'=8,'desc'=4] {'cell'}, dimensions={0}, use_global_device_ids=true | all-gather | bytes 73728 | tf_op jit(solution)/shard_map/all_gather | solution.py:11
  70.3 31.0 %all-gather.3 = f32[16384]{0:T(1024)S(1)} all-gather(f32[2048]{0:T(1024)S(1)} %exponential_reduce_fusion.6), channel_id=5, replica_groups=mesh['cell'=8,'desc'=4] {'cell'}, dimensions={0}, use_global_device_ids=true | all-gather | bytes 73728 | tf_op jit(solution)/shard_map/all_gather | solution.py:11
  105.9 4.4 exponential_reduce_fusion.5
  110.2 5.2 all-gather.4
  115.4 5.2 all-gather.5
  120.8 4.0 add_reduce_fusion.6
  124.8 4.3 exponential_reduce_fusion.4
  129.2 30.5 %all-gather.6 = f32[16384]{0:T(1024)S(1)} all-gather(f32[2048]{0:T(1024)S(1)} %add_reduce_fusion.6), channel_id=8, replica_groups=mesh['cell'=8,'desc'=4] {'cell'}, dimensions={0}, use_global_device_ids=true | all-gather | bytes 73728 | tf_op jit(solution)/shard_map/all_gather | solution.py:11
  159.7 30.5 %all-gather.7 = f32[16384]{0:T(1024)S(1)} all-gather(f32[2048]{0:T(1024)S(1)} %exponential_reduce_fusion.4), channel_id=9, replica_groups=mesh['cell'=8,'desc'=4] {'cell'}, dimensions={0}, use_global_device_ids=true | all-gather | bytes 73728 | tf_op jit(solution)/shard_map/all_gather | solution.py:11
  194.8 4.4 exponential_reduce_fusion.3
  199.1 5.2 all-gather.8
  204.3 5.2 all-gather.9
  209.7 4.0 add_reduce_fusion.5
  213.7 4.3 exponential_reduce_fusion.2
  218.0 30.5 %all-gather.10 = f32[16384]{0:T(1024)S(1)} all-gather(f32[2048]{0:T(1024)S(1)} %add_reduce_fusion.5), channel_id=12, replica_groups=mesh['cell'=8,'desc'=4] {'cell'}, dimensions={0}, use_global_device_ids=true | all-gather | bytes 73728 | tf_op jit(solution)/shard_map/all_gather | solution.py:11
  248.6 30.5 %all-gather.11 = f32[16384]{0:T(1024)S(1)} all-gather(f32[2048]{0:T(1024)S(1)} %exponential_reduce_fusion.2), channel_id=13, replica_groups=mesh['cell'=8,'desc'=4] {'cell'}, dimensions={0}, use_global_device_ids=true | all-gather | bytes 73728 | tf_op jit(solution)/shard_map/all_gather | solution.py:11
  279.6 4.0 add_reduce_fusion
  283.7 4.4 exponential_reduce_fusion.1
  288.0 5.2 all-gather.12
  293.3 5.4 all-gather.13
  298.8 4.0 add_reduce_fusion.4
  302.9 4.3 exponential_reduce_fusion
  307.2 30.5 %all-gather.14 = f32[16384]{0:T(1024)S(1)} all-gather(f32[2048]{0:T(1024)S(1)} %add_reduce_fusion.4), channel_id=16, replica_groups=mesh['cell'=8,'desc'=4] {'cell'}, dimensions={0}, use_global_device_ids=true | all-gather | bytes 73728 | tf_op jit(solution)/shard_map/all_gather | solution.py:11
  337.7 30.5 %all-gather.15 = f32[16384]{0:T(1024)S(1)} all-gather(f32[2048]{0:T(1024)S(1)} %exponential_reduce_fusion), channel_id=17, replica_groups=mesh['cell'=8,'desc'=4] {'cell'}, dimensions={0}, use_global_device_ids=true | all-gather | bytes 73728 | tf_op jit(solution)/shard_map/all_gather | solution.py:11
  368.8 4.5 multiply_reduce_fusion.3
  373.3 5.7 psum.56
  379.0 4.7 fusion
  383.7 21.5 %psum.57 = f32[2048]{0:T(1024)S(1)} all-reduce(f32[2048]{0:T(1024)S(1)} %fusion), channel_id=1, replica_groups=mesh['cell'=8,'desc'=4] {'cell'}, use_global_device_ids=true, to_apply=%region_35.36 | all-reduce | flops 2048 | bytes 16384 | tf_op jit(solution)/shard_map/psum | solution.py:80
  405.2 4.5 multiply_reduce_fusion.2
  409.7 5.7 psum.58
  415.4 4.6 fusion.1
  420.0 17.4 %psum.59 = f32[2048]{0:T(1024)S(1)} all-reduce(f32[2048]{0:T(1024)S(1)} %fusion.1), channel_id=1, replica_groups=mesh['cell'=8,'desc'=4] {'cell'}, use_global_device_ids=true, to_apply=%region_39.40 | all-reduce | flops 2048 | bytes 16384 | tf_op jit(solution)/shard_map/psum | solution.py:80
  437.4 4.5 multiply_reduce_fusion.1
  441.9 5.7 psum.60
  447.6 4.6 fusion.2
  452.3 19.4 %psum.61 = f32[2048]{0:T(1024)S(1)} all-reduce(f32[2048]{0:T(1024)S(1)} %fusion.2), channel_id=1, replica_groups=mesh['cell'=8,'desc'=4] {'cell'}, use_global_device_ids=true, to_apply=%region_43.44 | all-reduce | flops 2048 | bytes 16384 | tf_op jit(solution)/shard_map/psum | solution.py:80
  471.7 4.5 multiply_reduce_fusion
  476.2 5.7 psum.62
  481.8 24.6 %add_subtract_fusion = f32[1024,2048]{1,0:T(8,128)S(1)} fusion(f32[1024,2048]{1,0:T(8,128)} %copy-done.1, f32[1024]{0:T(1024)S(1)} %neg.59, f32[2048]{0:T(1024)S(1)} %get-tuple-element.338, f32[2048]{0:T(1024)S(1)} %neg.58, f32[1024]{0:T(1024)S(1)} %neg.57, f32[2048]{0:T(1024)S(1)} %get-tuple-element.340, f32[2048]{0:T(1024)S(1)} %neg.56, f32[1024]{0:T(1024)S(1)} %neg.55, ...), kind=kLoop, calls=%fused_computation.24 | loop fusion | flops 58720256 | bytes 16908288 | tf_op jit(solution)/shard_map/sub | solution.py:63
  506.4 13.4 %convolution_multiply_fusion.1 = f32[2048,256]{1,0:T(8,128)S(1)} fusion(f32[1024,2048]{1,0:T(8,128)S(1)} %add_subtract_fusion, f32[1024,256]{1,0:T(8,128)S(1)} %copy-done.3), kind=kOutput, calls=%fused_computation.56 | convolution fusion | flops 6442975232 | bytes 11534336 | tf_op jit(solution)/shard_map/dot_general | solution.py:83
  519.9 47.7 %collective-permute-done = f32[2048,256]{1,0:T(8,128)S(1)} collective-permute-done((f32[2048,256]{1,0:T(8,128)S(1)}, f32[2048,256]{1,0:T(8,128)S(1)}, u32[]{:S(2)}, u32[]{:S(2)}) %collective-permute-start) | collective-permute-done | bytes 2097184 | tf_op jit(solution)/shard_map/ppermute | solution.py:89
  568.0 46.9 %collective-permute-done.1 = f32[2048,256]{1,0:T(8,128)S(1)} collective-permute-done((f32[2048,256]{1,0:T(8,128)S(1)}, f32[2048,256]{1,0:T(8,128)S(1)}, u32[]{:S(2)}, u32[]{:S(2)}) %collective-permute-start.1) | collective-permute-done | bytes 2097184 | tf_op jit(solution)/shard_map/ppermute | solution.py:89
  616.5 7.6 %convolution_multiply_fusion.2 = f32[1024,256]{1,0:T(8,128)} fusion(f32[1024,2048]{1,0:T(8,128)S(1)} %add_subtract_fusion, f32[2048,256]{1,0:T(8,128)S(1)} %copy-done), kind=kOutput, calls=%fused_computation.57 | convolution fusion | flops 6442713088 | bytes 11534336 | tf_op jit(solution)/shard_map/dot_general | solution.py:82
  624.2 84.5 %collective-permute-done.2 = f32[2048,256]{1,0:T(8,128)} collective-permute-done((f32[2048,256]{1,0:T(8,128)}, f32[2048,256]{1,0:T(8,128)}, u32[]{:S(2)}, u32[]{:S(2)}) %collective-permute-start.2) | collective-permute-done | bytes 2097184 | tf_op jit(solution)/shard_map/ppermute | solution.py:89
  (179 shorter events, 26.9 us)
Async XLA Ops:
  7.2 1.6 copy-start
  7.2 16.9 %copy-start.4 = (f32[2048]{0:T(1024)S(1)}, f32[2048]{0:T(1024)}, u32[]{:S(2)}) copy-start(f32[2048]{0:T(1024)} %param.23) | copy-start | bytes 24580
  7.2 705.3 %all-reduce.2.cloned.1.call-start = ((), (), s32[]{:S(2)}) async-start(), calls=%async_computation | async-start | bytes 2097152 | tf_op jit(solution)/shard_map/psum | solution.py:86
  17.8 6.3 copy-start.1
  31.7 5.8 copy-start.2
  298.8 69.9 %copy-start.5 = (f32[2048]{0:T(1024)S(1)}, f32[2048]{0:T(1024)}, u32[]{:S(2)}) copy-start(f32[2048]{0:T(1024)} %param.25) | copy-start | bytes 24580
  302.9 76.1 %copy-start.6 = (f32[1024]{0:T(1024)S(1)}, f32[1024]{0:T(1024)}, u32[]{:S(2)}) copy-start(f32[1024]{0:T(1024)} %param.24) | copy-start | bytes 12292
  481.8 24.6 %copy-start.3 = (f32[1024,256]{1,0:T(8,128)S(1)}, f32[1024,256]{1,0:T(8,128)}, u32[]{:S(2)}) copy-start(f32[1024,256]{1,0:T(8,128)} %param.21) | copy-start | bytes 3145732
  519.9 47.8 %collective-permute-start = (f32[2048,256]{1,0:T(8,128)S(1)}, f32[2048,256]{1,0:T(8,128)S(1)}, u32[]{:S(2)}, u32[]{:S(2)}) collective-permute-start(f32[2048,256]{1,0:T(8,128)S(1)} %convolution_multiply_fusion.1), channel_id=1, source_target_pairs={{0,4},{4,0},{8,12},{12,8},{16,20},{20,16},{24,28},{28,24},{1,5},{5... | collective-permute-start | bytes 6291464 | tf_op jit(solution)/shard_map/ppermute | solution.py:89
  568.0 47.0 %collective-permute-start.1 = (f32[2048,256]{1,0:T(8,128)S(1)}, f32[2048,256]{1,0:T(8,128)S(1)}, u32[]{:S(2)}, u32[]{:S(2)}) collective-permute-start(f32[2048,256]{1,0:T(8,128)S(1)} %add.252), channel_id=1, source_target_pairs={{0,8},{4,12},{8,0},{12,4},{16,24},{20,28},{24,16},{28,20},{1,9},{5... | collective-permute-start | bytes 6291464 | tf_op jit(solution)/shard_map/ppermute | solution.py:89
  616.5 92.2 %collective-permute-start.2 = (f32[2048,256]{1,0:T(8,128)}, f32[2048,256]{1,0:T(8,128)}, u32[]{:S(2)}, u32[]{:S(2)}) collective-permute-start(f32[2048,256]{1,0:T(8,128)} %add.253), channel_id=1, source_target_pairs={{0,16},{4,20},{8,24},{12,28},{16,0},{20,4},{24,8},{28,12},{1,17},{... | collective-permute-start | bytes 6291464 | tf_op jit(solution)/shard_map/ppermute | solution.py:89
Sparse Core Ops, SparseCore 0:
  624.3 35.5 all-reduce.1
